TPU v7x, 32 devices: a whole 2x2x4 slice. The times are simulated.
32 devices in a mesh: slides: 2 (over y), tiles: 4 (over z), heads: 4 (over x, core).
Axes of the slice: x: 2, y: 2, z: 4, core: 2. Of those that a mesh axis runs over, the one named last changes fastest.
Arguments:
- pixels: bfloat16 [32, 4096, 192], P(('slides', 'tiles', 'heads')), parts along dimension 0, may hold values from -6 to 6
- w_stem: bfloat16 [192, 64], replicated, may hold values from -0.4375 to 0.4375
- w_conv1: bfloat16 [4, 9, 16, 32], replicated, may hold values from -0.5 to 0.5
- w_conv2: bfloat16 [4, 9, 32, 64], replicated, may hold values from -0.375 to 0.375
- w_key: bfloat16 [256, 512], P(None, 'heads'), may hold values from -0.375 to 0.375
- w_value: bfloat16 [256, 512], P(None, 'heads'), may hold values from -0.375 to 0.375
- queries: bfloat16 [512, 512], P(None, 'heads'), may hold values from -104 to 104
- tile_count: int32 [32], P(('slides', 'tiles', 'heads')), parts along dimension 0, may hold values from 0 to 1, as said below
- tissue: int32 [32], P(('slides', 'tiles', 'heads')), parts along dimension 0, may hold values from 17 to 256, as said below
- adjacency: int32 [32, 3], P(('slides', 'tiles', 'heads')), parts along dimension 0, may hold values from -1 to 0, as said below
Outputs:
- pooled: bfloat16 [1024, 512], P(('slides', 'tiles'), 'heads'), parts along dimension 0
There are 2 independent parts, one for each index of `slides`. A program takes and returns all parts, laid end to end along the dimension named above; an argument that names none is the same for every part. Nothing has to cross between parts.
Inputs may be any that keep to these rules, and one draw needn't show every extreme that they name: Device g (order of tiles+heads) holds tiles in its slots 0 to tile_count[g] - 1; the first device holds 1, the second 1; other devices may hold none. Tokens 0 to tissue[s] - 1 of slot s, raster order, are tissue; slot 0 is all tissue. `adjacency`: A code below 1 names a slot of the previous device along tiles+heads, a code c of 1 or more names slot c - 1 of the same device, earlier than the slot itself; -1 is background.
All inputs are finite; a program needn't handle non-finite values.
Results may differ from a plain program's by a relative error of at most 0.012.
The roundings to bfloat16 on the way count: a program that leaves them out, or rounds other values in their place, can miss the bound.
Values may be sent and summed in bfloat16 or wider, within the bound.
No kernel may reach another device: no remote copies, remote signals or barrier semaphores. Data moves between devices by JAX's collectives and lax.ppermute only.
A program may use at most 128 MiB of HBM per device.

v0:
```python
import jax
import jax.numpy as jnp
from jax import lax
from jax.sharding import PartitionSpec as P

STEM_GRID = 64
PATCH_DIM = 192
C_STEM = 64
C_OUT = 256
HEAD_DIM = 64
TOK_TILE = 256
NEG_BIG = -1e30
LN_EPS = 1e-05


def passed_along(block, axis, distance):
    devices = range(lax.axis_size(axis))
    route = [(i - distance, i) for i in devices if i - distance in devices]
    return lax.ppermute(block, axis, route)


def merged_2(array, axis, combine):
    everything = jax.tree.map(lambda part: lax.all_gather(part, axis), array)
    first = jax.tree.map(lambda part: part[0], everything)

    def lap(k, so_far):
        return combine(so_far, jax.tree.map(lambda part: part[k], everything))

    return lax.fori_loop(1, lax.axis_size(axis), lap, first)


def border_lines(feature_map):
    slot_n = feature_map.shape[0]
    side = feature_map.shape[1]
    channels = feature_map.shape[3]
    return jnp.stack([feature_map[:, side - 1], feature_map[:, :, side - 1]], axis=1).reshape(
        slot_n, 2, side * channels
    )


def bordered(inner, earlier, own_lines, adjacency):
    slot_n = inner.shape[0]
    side = inner.shape[1]
    channels = inner.shape[3]
    lines = jnp.concatenate([earlier, own_lines], axis=0)
    source_n = lines.shape[0]
    chooser = (
        adjacency[:, :, None] == jnp.arange(source_n, dtype=jnp.int32)[None, None, :]
    ).astype(jnp.bfloat16)
    above = (
        jnp.dot(chooser[:, 0], lines[:, 0], preferred_element_type=jnp.float32)
        .astype(jnp.bfloat16)
        .reshape(slot_n, side, channels)
    )
    beside = (
        jnp.dot(chooser[:, 1], lines[:, 1], preferred_element_type=jnp.float32)
        .astype(jnp.bfloat16)
        .reshape(slot_n, side, channels)
    )
    last_pixel = lines[:, 0].reshape(source_n, side, channels)[:, side - 1]
    corner = jnp.dot(chooser[:, 2], last_pixel, preferred_element_type=jnp.float32).astype(
        jnp.bfloat16
    )
    first_line = jnp.concatenate([corner[:, None], above], axis=1)
    lower = jnp.concatenate([beside[:, :, None], inner], axis=2)
    return jnp.concatenate([first_line[:, None], lower], axis=1)


def grouped_conv(padded, weight):
    groups_n = weight.shape[0]
    in_group = weight.shape[2]
    out_group = weight.shape[3]
    kernel = (
        weight.reshape(groups_n, 3, 3, in_group, out_group)
        .transpose(1, 2, 3, 0, 4)
        .reshape(3, 3, in_group, groups_n * out_group)
    )
    return lax.conv_general_dilated(
        padded,
        kernel,
        window_strides=(2, 2),
        padding="VALID",
        dimension_numbers=("NHWC", "HWIO", "NHWC"),
        feature_group_count=groups_n,
        preferred_element_type=jnp.float32,
    )


def partial_attention(query_heads, key_rows, value_rows, valid_rows):
    scores = jnp.einsum(
        "lhd,thd->hlt", query_heads, key_rows, preferred_element_type=jnp.float32
    ) * float(HEAD_DIM) ** (-0.5)
    scores = jnp.where(valid_rows[None, None, :] > 0.5, scores, NEG_BIG)
    row_peak = jnp.max(scores, axis=2)
    weights = jnp.exp(scores - row_peak[:, :, None]) * valid_rows[None, None, :]
    totals = jnp.sum(weights, axis=2)
    weighted = jnp.einsum(
        "hlt,thd->lhd", weights.astype(jnp.bfloat16), value_rows, preferred_element_type=jnp.float32
    )
    latent_n = query_heads.shape[0]
    return (row_peak.T, totals.T, weighted.reshape(latent_n, -1))


def softmax_merge(first, second):
    joint = jnp.maximum(first[0], second[0])
    scale_one = jnp.exp(first[0] - joint)
    scale_two = jnp.exp(second[0] - joint)
    totals = first[1] * scale_one + second[1] * scale_two
    weighted = first[2] * jnp.repeat(scale_one, HEAD_DIM, axis=1) + second[2] * jnp.repeat(
        scale_two, HEAD_DIM, axis=1
    )
    return (joint, totals, weighted)


def per_device(
    pixels, w_stem, w_conv1, w_conv2, w_key, w_value, queries, tile_count, tissue, adjacency
):
    slot_n = pixels.shape[0]
    slot_live = (jnp.arange(slot_n, dtype=jnp.int32) < tile_count[0]).astype(jnp.float32)
    stem_flat = jnp.dot(
        pixels.reshape(slot_n * STEM_GRID * STEM_GRID, PATCH_DIM),
        w_stem,
        preferred_element_type=jnp.float32,
    )
    stem_map = (
        jnp.maximum(stem_flat, 0.0).reshape(slot_n, STEM_GRID, STEM_GRID, C_STEM)
        * slot_live[:, None, None, None]
    ).astype(jnp.bfloat16)
    stem_lines = border_lines(stem_map)
    stem_prior = passed_along(stem_lines, ("tiles", "heads"), 1)
    middle = grouped_conv(bordered(stem_map, stem_prior, stem_lines, adjacency), w_conv1)
    middle = (jnp.maximum(middle, 0.0) * slot_live[:, None, None, None]).astype(jnp.bfloat16)
    middle_lines = border_lines(middle)
    middle_prior = passed_along(middle_lines, ("tiles", "heads"), 1)
    deepest = jnp.maximum(
        grouped_conv(bordered(middle, middle_prior, middle_lines, adjacency), w_conv2), 0.0
    )
    token_n = slot_n * TOK_TILE
    deepest = deepest.reshape(token_n, C_OUT)
    centred = deepest - jnp.mean(deepest, axis=1, keepdims=True)
    normed = (
        centred * lax.rsqrt(jnp.mean(centred * centred, axis=1, keepdims=True) + LN_EPS)
    ).astype(jnp.bfloat16)
    in_tile = (jnp.arange(TOK_TILE, dtype=jnp.int32)[None, :] < tissue[:, None]).astype(jnp.float32)
    valid = (in_tile * slot_live[:, None]).reshape(token_n).astype(jnp.bfloat16)
    latent_n = queries.shape[0]
    head_local = queries.shape[1] // HEAD_DIM
    head_width = head_local * HEAD_DIM
    weight_both = jnp.concatenate([w_key, w_value], axis=1)
    query_heads = queries.reshape(latent_n, head_local, HEAD_DIM)

    def attend_rows(running, normed_rows, valid_rows):
        projected = jnp.dot(normed_rows, weight_both, preferred_element_type=jnp.float32).astype(
            jnp.bfloat16
        )
        key_rows = projected[:, :head_width].reshape(-1, head_local, HEAD_DIM)
        value_rows = projected[:, head_width:].reshape(-1, head_local, HEAD_DIM)
        return softmax_merge(
            running, partial_attention(query_heads, key_rows, value_rows, valid_rows)
        )

    start_state = (
        jnp.full((latent_n, head_local), NEG_BIG, jnp.float32),
        jnp.zeros((latent_n, head_local), jnp.float32),
        jnp.zeros((latent_n, head_width), jnp.float32),
    )
    normed_rows = lax.all_gather(normed, "heads", axis=0, tiled=True)
    valid_rows = lax.all_gather(valid, "heads", axis=0, tiled=True)
    row_total = normed_rows.shape[0]
    blocks = (
        normed_rows.reshape(row_total // token_n, token_n, C_OUT),
        valid_rows.reshape(row_total // token_n, token_n),
    )

    def scan_step(inner_state, block_pair):
        return (attend_rows(inner_state, block_pair[0], block_pair[1]), None)

    softmax_state = lax.scan(scan_step, start_state, blocks)[0]
    tile_n = lax.axis_size("tiles")
    share = latent_n // tile_n
    merged = merged_2(softmax_state, "tiles", softmax_merge)
    first_row = lax.axis_index("tiles") * share
    totals = lax.dynamic_slice_in_dim(merged[1], first_row, share, 0)
    weighted = lax.dynamic_slice_in_dim(merged[2], first_row, share, 0)
    return (weighted / jnp.repeat(totals, HEAD_DIM, axis=1)).astype(jnp.bfloat16)


def solution(mesh):
    in_specs = (
        P(("slides", "tiles", "heads"), None, None),
        P(),
        P(),
        P(),
        P(None, "heads"),
        P(None, "heads"),
        P(None, "heads"),
        P(("slides", "tiles", "heads")),
        P(("slides", "tiles", "heads")),
        P(("slides", "tiles", "heads"), None),
    )
    out_specs = P(("slides", "tiles"), "heads")
    return jax.shard_map(
        per_device, mesh=mesh, in_specs=in_specs, out_specs=out_specs, check_vma=False
    )
```

profile of v0, /device:TPU:0, one launch (start us, length us, event | category | flops | bytes accessed | tf_op | source)
XLA Modules:
  0.0 160.6 jit_solution(8616740887920046742)
XLA Ops:
  10.3 1.4 slice.83
  11.7 2.4 %copy.115 = bf16[1,64,1,64]{3,1,2,0:T(8,128)(2,1)S(1)} copy(bf16[1,64,1,64]{2,1,3,0:T(8,128)(2,1)} %slice.83) | data formatting | bytes 16384
  14.5 2.4 %collective-permute-start = (bf16[1,2,4096]{2,1,0:T(2,128)(2,1)S(1)}, bf16[1,2,4096]{2,1,0:T(2,128)(2,1)S(1)}, u32[]{:S(2)}, u32[]{:S(2)}) collective-permute-start(bf16[1,2,4096]{2,1,0:T(2,128)(2,1)S(1)} %pad_maximum_fusion.2), channel_id=1, source_target_pairs={{0,1},{1,2},{2,3},{3,4},{4,5},{5,6},{6,7},{7,8},{8,9},{9,10},{10,1... | collective-permute-start | bytes 49160 | tf_op jit(solution)/shard_map/ppermute | solution.py:19
  16.9 2.1 %convert_element_type.97 = bf16[1,64,64,4,16]{2,1,4,3,0:T(8,128)(2,1)} reshape(bf16[4096,64]{0,1:T(8,128)(2,1)S(1)} %fusion.19) | data formatting | bytes 1048576 | tf_op jit(solution)/shard_map/convert_element_type | solution.py:128
  19.1 2.9 %copy.91 = bf16[1,64,64,4,16]{2,4,3,1,0:T(8,128)(2,1)} copy(bf16[1,64,64,4,16]{2,1,4,3,0:T(8,128)(2,1)} %convert_element_type.97) | data formatting | bytes 1048576 | tf_op jit(solution)/shard_map/convert_element_type | solution.py:128
  23.0 3.2 %concatenate.63 = bf16[1,64,1,4,16]{2,4,3,1,0:T(8,128)(2,1)} reshape(bf16[4096]{0:T(1024)(128)(2,1)S(1)} %convert_element_type.96) | data formatting | bytes 16384 | tf_op jit(solution)/shard_map/concatenate | solution.py:65
  26.9 2.1 %maximum_maximum_fusion.1 = bf16[1,65,65,4,16]{2,4,3,1,0:T(8,128)(2,1)S(1)} fusion(bf16[1,64,64,4,16]{2,4,3,1,0:T(8,128)(2,1)} %copy.91, bf16[1,64,1,4,16]{2,4,3,1,0:T(8,128)(2,1)} %concatenate.63, bf16[1,1,64,4,16]{2,4,3,1,0:T(8,128)(2,1)S(1)} %copy.89, bf16[1,1,1,4,16]{2,4,3,1,0:T(8,128)(2,1)S(1)} %concatenate.62), kind=kLoop, calls=%fused_computation.51 | loop fusion | flops 2163200 | bytes 1081600 | tf_op jit(solution)/shard_map/concatenate | solution.py:66
  29.0 13.2 %copy.92 = bf16[1,65,65,4,16]{4,0,3,2,1:T(2,128)(2,1)} copy(bf16[1,65,65,4,16]{2,4,3,1,0:T(8,128)(2,1)S(1)} %maximum_maximum_fusion.1) | data formatting | bytes 1081600 | tf_op jit(solution)/shard_map/concatenate | solution.py:66
  42.2 22.5 %fusion.39 = (bf16[32,32,4,32]{3,2,1,0:T(4,128)(2,1)S(1)}, bf16[1,32,32,4,32]{4,0,3,2,1:T(2,128)(2,1)}) fusion(f32[]{:T(128)} %bitcast.6, bf16[1,65,65,4,16]{4,0,3,2,1:T(2,128)(2,1)} %copy.92, bf16[4,3,3,16,32]{4,3,2,1,0:T(8,128)(2,1)S(1)} %bitcast.205), kind=kOutput, calls=%fused_computation.90 | convolution fusion | flops 38141952 | bytes 1101956 | tf_op jit(solution)/shard_map/conv_general_dilated | solution.py:78
  65.3 4.5 %collective-permute-start.1 = (bf16[1,2,4096]{2,0,1:T(2,128)(2,1)S(1)}, bf16[1,2,4096]{2,0,1:T(2,128)(2,1)S(1)}, u32[]{:S(2)}, u32[]{:S(2)}) collective-permute-start(bf16[1,2,4096]{2,0,1:T(2,128)(2,1)S(1)} %pad_maximum_fusion.1), channel_id=1, source_target_pairs={{0,1},{1,2},{2,3},{3,4},{4,5},{5,6},{6,7},{7,8},{8,9},{9,10},{10,1... | collective-permute-start | bytes 49160 | tf_op jit(solution)/shard_map/ppermute | solution.py:19
  69.9 5.1 %all-gather.3 = bf16[4,1,256]{2,1,0:T(2,128)(2,1)S(1)} all-gather(bf16[1,1,256]{2,1,0:T(2,128)(2,1)S(1)} %reshape.325), channel_id=1, replica_groups=mesh['slides'=2,'tiles'=4,'heads'=4] {'heads'}, dimensions={0}, use_global_device_ids=true | all-gather | bytes 2560 | tf_op jit(solution)/shard_map/all_gather | solution.py:168
  75.1 5.2 %copy.99 = bf16[1,32,32,4,32]{2,4,3,1,0:T(8,128)(2,1)S(1)} copy(bf16[1,32,32,4,32]{4,0,3,2,1:T(2,128)(2,1)} %get-tuple-element.341) | data formatting | bytes 524288 | tf_op jit(solution)/shard_map/convert_element_type | solution.py:132
  80.8 3.1 %concatenate.65 = bf16[1,32,1,4,32]{2,4,3,1,0:T(8,128)(2,1)} reshape(bf16[4096]{0:T(1024)(128)(2,1)S(1)} %convert_element_type.102) | data formatting | bytes 16384 | tf_op jit(solution)/shard_map/concatenate | solution.py:65
  84.5 2.8 %maximum_maximum_fusion = bf16[1,33,33,4,32]{2,4,3,1,0:T(8,128)(2,1)} fusion(bf16[1,32,32,4,32]{2,4,3,1,0:T(8,128)(2,1)S(1)} %copy.99, bf16[1,32,1,4,32]{2,4,3,1,0:T(8,128)(2,1)} %concatenate.65, bf16[1,1,32,4,32]{2,4,3,1,0:T(8,128)(2,1)S(1)} %copy.97, bf16[1,1,1,4,32]{2,4,3,1,0:T(8,128)(2,1)S(1)} %concatenate.64), kind=kLoop, calls=%fused_computation.50 | loop fusion | flops 1115136 | bytes 557568 | tf_op jit(solution)/shard_map/concatenate | solution.py:66
  87.3 6.1 %copy.100 = bf16[1,33,33,4,32]{4,0,3,2,1:T(2,128)(2,1)} copy(bf16[1,33,33,4,32]{2,4,3,1,0:T(8,128)(2,1)} %maximum_maximum_fusion) | data formatting | bytes 557568 | tf_op jit(solution)/shard_map/concatenate | solution.py:66
  93.4 5.4 %fusion.40 = (f32[16,16]{1,0:T(8,128)S(1)}, f32[1,16,16,4,64]{4,0,3,2,1:T(1,128)S(1)}) fusion(bf16[1,33,33,4,32]{4,0,3,2,1:T(2,128)(2,1)} %copy.100, bf16[4,3,3,32,64]{4,3,2,1,0:T(8,128)(2,1)S(1)} %bitcast.204), kind=kOutput, calls=%fused_computation.91 | convolution fusion | flops 37879552 | bytes 689408 | tf_op jit(solution)/shard_map/conv_general_dilated | solution.py:78
  99.5 3.4 %multiply_reduce_fusion = (f32[16,16]{1,0:T(8,128)S(1)}, f32[16,16,4,64]{3,2,1,0:T(4,128)S(1)}) fusion(f32[1,16,16,4,64]{4,0,3,2,1:T(1,128)S(1)} %get-tuple-element.343, f32[16,16]{1,0:T(8,128)S(1)} %broadcast_multiply_fusion, f32[]{:T(128)} %broadcast.180), kind=kLoop, calls=%fused_computation.52 | loop fusion | flops 196352 | bytes 526340 | tf_op jit(solution)/shard_map/reduce_sum | solution.py:142
  103.5 7.7 %all_gather.25 = bf16[1024,256]{1,0:T(8,128)(2,1)} all-gather(bf16[256,256]{1,0:T(8,128)(2,1)S(1)} %multiply_convert_fusion), channel_id=1, replica_groups=mesh['slides'=2,'tiles'=4,'heads'=4] {'heads'}, dimensions={0}, use_global_device_ids=true | all-gather | bytes 655360 | tf_op jit(solution)/shard_map/all_gather | solution.py:167
  111.2 9.0 %while.35 = (s32[]{:T(128)}, f32[512,2]{0,1:T(2,128)S(1)}, f32[512,2]{0,1:T(2,128)S(1)}, f32[512,128]{0,1:T(8,128)S(1)}, bf16[4,256]{1,0:T(4,128)(2,1)S(1)}, /*i...) while((s32[]{:T(128)}, f32[512,2]{0,1:T(2,128)S(1)}, ...), condition=%wide.region_5.6_spmd.clone, body=%wide.region_2.5_spmd.clone.sunk | while | flops 103357440 | bytes 5174392 | solution.py:178
  121.0 13.4 %all-gather = f32[2048,2]{0,1:T(2,128)S(1)} all-gather(f32[512,2]{0,1:T(2,128)S(1)} %get-tuple-element.226), channel_id=2, replica_groups=mesh['slides'=2,'tiles'=4,'heads'=4] {'tiles'}, dimensions={0}, use_global_device_ids=true | all-gather | bytes 20480 | tf_op jit(solution)/shard_map/all_gather | solution.py:23
  134.3 13.3 %all-gather.1 = f32[2048,2]{0,1:T(2,128)S(1)} all-gather(f32[512,2]{0,1:T(2,128)S(1)} %get-tuple-element.227), channel_id=3, replica_groups=mesh['slides'=2,'tiles'=4,'heads'=4] {'tiles'}, dimensions={0}, use_global_device_ids=true | all-gather | bytes 20480 | tf_op jit(solution)/shard_map/all_gather | solution.py:23
  147.6 2.1 %all-gather.6.cloned.1.call-done = f32[2048,128]{0,1:T(8,128)} async-done(((f32[512,128]{0,1:T(8,128)}), f32[2048,128]{0,1:T(8,128)}) %all-gather.6.cloned.1.call-update) | async-done | bytes 1048592 | tf_op jit(solution)/shard_map/all_gather | solution.py:23
  149.7 2.0 %reshape.318 = f32[4,512,128]{1,0,2:T(4,128)S(1)} reshape(f32[2048,128]{0,1:T(8,128)} %all-gather.6.cloned.1.call-done) | data formatting | bytes 2097152 | tf_op jit(solution)/shard_map/all_gather | solution.py:23
  151.7 1.2 while.34
  (124 shorter events, 18.7 us)
Async XLA Ops:
  6.5 1.4 copy-start
  6.5 143.2 %all-gather.6.cloned.1.call-start = ((), (), s32[]{:S(2)}) async-start(), calls=%async_computation | async-start | bytes 1310720 | tf_op jit(solution)/shard_map/all_gather | solution.py:23
  9.1 7.7 %copy-start.7 = (s32[1,3]{1,0:T(1,128)S(1)}, s32[1,3]{1,0:T(1,128)}, u32[]{:S(2)}) copy-start(s32[1,3]{1,0:T(1,128)} %param.23) | copy-start | bytes 40
  9.1 7.8 %copy-start.3 = (bf16[256,128]{1,0:T(8,128)(2,1)S(1)}, bf16[256,128]{1,0:T(8,128)(2,1)}, u32[]{:S(2)}) copy-start(bf16[256,128]{1,0:T(8,128)(2,1)} %param.19) | copy-start | bytes 196612
  9.2 7.8 %copy-start.4 = (bf16[256,128]{1,0:T(8,128)(2,1)S(1)}, bf16[256,128]{1,0:T(8,128)(2,1)}, u32[]{:S(2)}) copy-start(bf16[256,128]{1,0:T(8,128)(2,1)} %param.18) | copy-start | bytes 196612
  14.5 8.1 %collective-permute-start = (bf16[1,2,4096]{2,1,0:T(2,128)(2,1)S(1)}, bf16[1,2,4096]{2,1,0:T(2,128)(2,1)S(1)}, u32[]{:S(2)}, u32[]{:S(2)}) collective-permute-start(bf16[1,2,4096]{2,1,0:T(2,128)(2,1)S(1)} %pad_maximum_fusion.2), channel_id=1, source_target_pairs={{0,1},{1,2},{2,3},{3,4},{4,5},{5,6},{6,7},{7,8},{8,9},{9,10},{10,1... | collective-permute-start | bytes 49160 | tf_op jit(solution)/shard_map/ppermute | solution.py:19
  29.0 13.2 %copy-start.6 = (bf16[4,9,16,32]{3,2,1,0:T(8,128)(2,1)S(1)}, bf16[4,9,16,32]{3,2,1,0:T(8,128)(2,1)}, u32[]{:S(2)}) copy-start(bf16[4,9,16,32]{3,2,1,0:T(8,128)(2,1)} %param.16) | copy-start | bytes 110596
  42.2 32.7 %copy-start.2 = (bf16[512,128]{1,0:T(8,128)(2,1)S(1)}, bf16[512,128]{1,0:T(8,128)(2,1)}, u32[]{:S(2)}) copy-start(bf16[512,128]{1,0:T(8,128)(2,1)} %param.20) | copy-start | bytes 393220
  65.3 15.0 %collective-permute-start.1 = (bf16[1,2,4096]{2,0,1:T(2,128)(2,1)S(1)}, bf16[1,2,4096]{2,0,1:T(2,128)(2,1)S(1)}, u32[]{:S(2)}, u32[]{:S(2)}) collective-permute-start(bf16[1,2,4096]{2,0,1:T(2,128)(2,1)S(1)} %pad_maximum_fusion.1), channel_id=1, source_target_pairs={{0,1},{1,2},{2,3},{3,4},{4,5},{5,6},{6,7},{7,8},{8,9},{9,10},{10,1... | collective-permute-start | bytes 49160 | tf_op jit(solution)/shard_map/ppermute | solution.py:19
  87.3 6.1 %copy-start.5 = (bf16[4,9,32,64]{3,2,1,0:T(8,128)(2,1)S(1)}, bf16[4,9,32,64]{3,2,1,0:T(8,128)(2,1)}, u32[]{:S(2)}) copy-start(bf16[4,9,32,64]{3,2,1,0:T(8,128)(2,1)} %param.17) | copy-start | bytes 442372
  120.2 0.7 copy-start.1
  149.7 2.0 %slice-start = ((f32[2048,128]{0,1:T(8,128)}), f32[512,128]{0,1:T(8,128)S(1)}, s32[]{:S(2)}) async-start(f32[2048,128]{0,1:T(8,128)} %all-gather.6.cloned.1.call-done), calls=%async_computation.1 | async-start | bytes 524288 | tf_op jit(solution)/shard_map/slice | solution.py:24
Sparse Core Ops, SparseCore 0:
  121.1 28.5 all-gather.5
where the time goes:
time: 161 us
  local copies, waits for them, and re-layouts  48.7 us (30%)
  blocking collectives  39.4 us (24%)
  matrix products  37.1 us (23%)
  between operations  15.2 us (9%)
  other arithmetic  10.8 us (7%)
  starting transfers between devices  6.87 us (4%)
  waiting for transfers between devices  2.12 us (1%)
    conv_general_dilated x2, matrix products, grouped_conv(): lax.conv_general_dilated(padded, kernel, window_strides=(2, 2), padding='...  27.9 us
    all_gather x2, blocking collectives, merged_2(): everything = jax.tree.map(lambda part: lax.all_gather(part, axis), array)  26.6 us
    concatenate x2, local copies, waits for them, and re-layouts, bordered(): return jnp.concatenate([first_line[:, None], lower], axis=1)  19.3 us
    all_gather x1, blocking collectives, per_device(): normed_rows = lax.all_gather(normed, 'heads', axis=0, tiled=True)  7.71 us
    ppermute x2, starting transfers between devices, passed_along(): return lax.ppermute(block, axis, route)  6.87 us
    concatenate x2, local copies, waits for them, and re-layouts, bordered(): lower = jnp.concatenate([beside[:, :, None], inner], axis=2)  6.28 us
    convert_element_type x3, local copies, waits for them, and re-layouts, per_device(): stem_map = (jnp.maximum(stem_flat, 0.0).reshape(slot_n, STEM_GRID, STEM_G...  6.14 us
    convert_element_type x2, local copies, waits for them, and re-layouts, per_device(): (jnp.maximum(middle, 0.0) * slot_live[:, None, None, None]).astype(jnp.bf...  5.74 us
  transfers between devices with their start and end apart: 3, of which 1 were waited for; matrix products, arithmetic and copies ran while one was open for 7% of the time, Pallas kernels for 0%

commit v1 on v0

--- a/solution.py
+++ b/solution.py
@@ -11,6 +11,21 @@
 TOK_TILE = 256
 NEG_BIG = -1e30
 LN_EPS = 1e-05
+
+
+def _expand_modes(block_here):
+    axis_id = "heads"
+    v_next, then, local_now = (lax.psum(1, axis_id), lax.axis_index(axis_id), block_here.shape[0])
+    f_now, mid_arr = (block_here, 1)
+    while mid_arr < v_next:
+        cards = []
+        kk = 0
+        while kk < v_next:
+            cards.append((kk, (kk - mid_arr) % v_next))
+            kk += 1
+        f_now = jnp.concatenate([f_now, lax.ppermute(f_now, axis_id, cards)], 0)
+        mid_arr = 2 * mid_arr
+    return jnp.roll(f_now, then * local_now, 0)
 
 
 def passed_along(block, axis, distance):
@@ -164,7 +179,7 @@
         jnp.zeros((latent_n, head_local), jnp.float32),
         jnp.zeros((latent_n, head_width), jnp.float32),
     )
-    normed_rows = lax.all_gather(normed, "heads", axis=0, tiled=True)
+    normed_rows = _expand_modes(normed)
     valid_rows = lax.all_gather(valid, "heads", axis=0, tiled=True)
     row_total = normed_rows.shape[0]
     blocks = (

time: 161 us -> 163 us (1.012)
  blocking collectives: 39.4 us -> 36.1 us
  starting transfers between devices: 6.87 us -> 9.27 us
  local copies, waits for them, and re-layouts: 48.7 us -> 50.5 us
    all_gather x1 -> x0, blocking collectives: 7.71 us -> none  [per_device(): normed_rows = lax.all_gather(normed, 'heads', axis=0, tiled=True)]
    all_gather x1, blocking collectives: 5.07 us -> 9.53 us  [per_device(): valid_rows = lax.all_gather(valid, 'heads', axis=0, tiled=True)]
    unnamed x23 -> x27, local copies, waits for them, and re-layouts: 4.03 us -> 6.71 us
    ppermute x0 -> x2, starting transfers between devices: none -> 2.4 us  [_expand_modes(): f_now = jnp.concatenate([f_now, lax.ppermute(f_now, axis_id, cards)], 0)]
    convert_element_type x3, local copies, waits for them, and re-layouts: 6.14 us -> 3.9 us  [per_device(): stem_map = (jnp.maximum(stem_flat, 0.0).reshape(slot_n, STEM_GRID, STEM_G...]
    dynamic_slice x0 -> x1, local copies, waits for them, and re-layouts: none -> 1.88 us  [_expand_modes(): return jnp.roll(f_now, then * local_now, 0)]
    ppermute x0 -> x2, waiting for transfers between devices: none -> 1.87 us  [_expand_modes(): f_now = jnp.concatenate([f_now, lax.ppermute(f_now, axis_id, cards)], 0)]
  transfers between devices with their start and end apart: 3 -> 5, of which waited for: 1 -> 2; matrix products, arithmetic and copies ran while one was open for 7% -> 6% of each run, Pallas kernels for 0% -> 0%
where the time goes in v1:
time: 163 us; the launch traced here: 162 us
  local copies, waits for them, and re-layouts  50.5 us (31%)
  matrix products  37.1 us (23%)
  blocking collectives  36.1 us (22%)
  between operations  15.3 us (9%)
  other arithmetic  10.8 us (7%)
  starting transfers between devices  9.27 us (6%)
  waiting for transfers between devices  3.06 us (2%)
    conv_general_dilated x2, matrix products, grouped_conv(): lax.conv_general_dilated(padded, kernel, window_strides=(2, 2), padding='...  27.9 us
    all_gather x2, blocking collectives, merged_2(): everything = jax.tree.map(lambda part: lax.all_gather(part, axis), array)  26.6 us
    concatenate x2, local copies, waits for them, and re-layouts, bordered(): return jnp.concatenate([first_line[:, None], lower], axis=1)  17.9 us
    all_gather x1, blocking collectives, per_device(): valid_rows = lax.all_gather(valid, 'heads', axis=0, tiled=True)  9.53 us
    ppermute x2, starting transfers between devices, passed_along(): return lax.ppermute(block, axis, route)  6.87 us
    unnamed x27, local copies, waits for them, and re-layouts  6.71 us
    concatenate x2, local copies, waits for them, and re-layouts, bordered(): lower = jnp.concatenate([beside[:, :, None], inner], axis=2)  6.25 us
    convert_element_type x2, local copies, waits for them, and re-layouts, per_device(): (jnp.maximum(middle, 0.0) * slot_live[:, None, None, None]).astype(jnp.bf...  6.06 us
  transfers between devices with their start and end apart: 5, of which 2 were waited for; matrix products, arithmetic and copies ran while one was open for 6% of the time, Pallas kernels for 0%

profile of v1, /device:TPU:0, one launch (start us, length us, event | category | flops | bytes accessed | tf_op | source)
XLA Modules:
  0.0 162.4 jit_solution(240375965372454754)
XLA Ops:
  10.3 1.4 slice.83
  11.7 2.4 %copy.115 = bf16[1,64,1,64]{3,1,2,0:T(8,128)(2,1)S(1)} copy(bf16[1,64,1,64]{2,1,3,0:T(8,128)(2,1)} %slice.83) | data formatting | bytes 16384
  14.4 2.4 %collective-permute-start = (bf16[1,2,4096]{2,1,0:T(2,128)(2,1)S(1)}, bf16[1,2,4096]{2,1,0:T(2,128)(2,1)S(1)}, u32[]{:S(2)}, u32[]{:S(2)}) collective-permute-start(bf16[1,2,4096]{2,1,0:T(2,128)(2,1)S(1)} %pad_maximum_fusion.3), channel_id=1, source_target_pairs={{0,1},{1,2},{2,3},{3,4},{4,5},{5,6},{6,7},{7,8},{8,9},{9,10},{10,1... | collective-permute-start | bytes 49160 | tf_op jit(solution)/shard_map/ppermute | solution.py:34
  18.0 1.6 %copy.91 = bf16[1,64,64,4,16]{2,4,3,1,0:T(8,128)(2,1)} copy(bf16[1,64,64,4,16]{2,1,4,3,0:T(8,128)(2,1)S(1)} %convert_element_type.97) | data formatting | bytes 1048576 | tf_op jit(solution)/shard_map/convert_element_type | solution.py:143
  20.0 3.2 %concatenate.75 = bf16[1,64,1,4,16]{2,4,3,1,0:T(8,128)(2,1)} reshape(bf16[4096]{0:T(1024)(128)(2,1)S(1)} %convert_element_type.96) | data formatting | bytes 16384 | tf_op jit(solution)/shard_map/concatenate | solution.py:80
  23.9 2.1 %maximum_maximum_fusion.1 = bf16[1,65,65,4,16]{2,4,3,1,0:T(8,128)(2,1)S(1)} fusion(bf16[1,64,64,4,16]{2,4,3,1,0:T(8,128)(2,1)} %copy.91, bf16[1,64,1,4,16]{2,4,3,1,0:T(8,128)(2,1)} %concatenate.75, bf16[1,1,64,4,16]{2,4,3,1,0:T(8,128)(2,1)S(1)} %copy.89, bf16[1,1,1,4,16]{2,4,3,1,0:T(8,128)(2,1)S(1)} %concatenate.74), kind=kLoop, calls=%fused_computation.51 | loop fusion | flops 2163200 | bytes 1081600 | tf_op jit(solution)/shard_map/concatenate | solution.py:81
  26.1 13.1 %copy.92 = bf16[1,65,65,4,16]{4,0,3,2,1:T(2,128)(2,1)} copy(bf16[1,65,65,4,16]{2,4,3,1,0:T(8,128)(2,1)S(1)} %maximum_maximum_fusion.1) | data formatting | bytes 1081600 | tf_op jit(solution)/shard_map/concatenate | solution.py:81
  39.2 22.4 %fusion.39 = (bf16[32,32,4,32]{3,2,1,0:T(4,128)(2,1)S(1)}, bf16[1,32,32,4,32]{4,0,3,2,1:T(2,128)(2,1)}) fusion(f32[]{:T(128)} %bitcast.6, bf16[1,65,65,4,16]{4,0,3,2,1:T(2,128)(2,1)} %copy.92, bf16[4,3,3,16,32]{4,3,2,1,0:T(8,128)(2,1)S(1)} %bitcast.205), kind=kOutput, calls=%fused_computation.98 | convolution fusion | flops 38141952 | bytes 1101956 | tf_op jit(solution)/shard_map/conv_general_dilated | solution.py:93
  62.2 4.5 %collective-permute-start.1 = (bf16[1,2,4096]{2,0,1:T(2,128)(2,1)S(1)}, bf16[1,2,4096]{2,0,1:T(2,128)(2,1)S(1)}, u32[]{:S(2)}, u32[]{:S(2)}) collective-permute-start(bf16[1,2,4096]{2,0,1:T(2,128)(2,1)S(1)} %pad_maximum_fusion.2), channel_id=1, source_target_pairs={{0,1},{1,2},{2,3},{3,4},{4,5},{5,6},{6,7},{7,8},{8,9},{9,10},{10,1... | collective-permute-start | bytes 49160 | tf_op jit(solution)/shard_map/ppermute | solution.py:34
  66.7 5.6 %copy.99 = bf16[1,32,32,4,32]{2,4,3,1,0:T(8,128)(2,1)} copy(bf16[1,32,32,4,32]{4,0,3,2,1:T(2,128)(2,1)} %get-tuple-element.343) | data formatting | bytes 524288 | tf_op jit(solution)/shard_map/convert_element_type | solution.py:147
  72.7 3.1 %concatenate.77 = bf16[1,32,1,4,32]{2,4,3,1,0:T(8,128)(2,1)} reshape(bf16[4096]{0:T(1024)(128)(2,1)S(1)} %convert_element_type.102) | data formatting | bytes 16384 | tf_op jit(solution)/shard_map/concatenate | solution.py:80
  76.4 2.1 %maximum_maximum_fusion = bf16[1,33,33,4,32]{2,4,3,1,0:T(8,128)(2,1)S(1)} fusion(bf16[1,32,32,4,32]{2,4,3,1,0:T(8,128)(2,1)} %copy.99, bf16[1,32,1,4,32]{2,4,3,1,0:T(8,128)(2,1)} %concatenate.77, bf16[1,1,32,4,32]{2,4,3,1,0:T(8,128)(2,1)S(1)} %copy.97, bf16[1,1,1,4,32]{2,4,3,1,0:T(8,128)(2,1)S(1)} %concatenate.76), kind=kLoop, calls=%fused_computation.50 | loop fusion | flops 1115136 | bytes 557568 | tf_op jit(solution)/shard_map/concatenate | solution.py:81
  78.5 4.8 %copy.100 = bf16[1,33,33,4,32]{4,0,3,2,1:T(2,128)(2,1)} copy(bf16[1,33,33,4,32]{2,4,3,1,0:T(8,128)(2,1)S(1)} %maximum_maximum_fusion) | data formatting | bytes 557568 | tf_op jit(solution)/shard_map/concatenate | solution.py:81
  83.3 5.4 %fusion.40 = (f32[16,16]{1,0:T(8,128)S(1)}, f32[1,16,16,4,64]{4,0,3,2,1:T(1,128)S(1)}) fusion(bf16[1,33,33,4,32]{4,0,3,2,1:T(2,128)(2,1)} %copy.100, bf16[4,3,3,32,64]{4,3,2,1,0:T(8,128)(2,1)S(1)} %bitcast.204), kind=kOutput, calls=%fused_computation.99 | convolution fusion | flops 37879552 | bytes 689408 | tf_op jit(solution)/shard_map/conv_general_dilated | solution.py:93
  89.4 3.4 %multiply_reduce_fusion = (f32[16,16]{1,0:T(8,128)S(1)}, f32[16,16,4,64]{3,2,1,0:T(4,128)S(1)}) fusion(f32[1,16,16,4,64]{4,0,3,2,1:T(1,128)S(1)} %get-tuple-element.345, f32[16,16]{1,0:T(8,128)S(1)} %broadcast_multiply_fusion, f32[]{:T(128)} %broadcast.181), kind=kLoop, calls=%fused_computation.52 | loop fusion | flops 196352 | bytes 526340 | tf_op jit(solution)/shard_map/reduce_sum | solution.py:157
  94.0 2.3 %collective-permute-start.2 = (bf16[256,256]{1,0:T(8,128)(2,1)S(1)}, bf16[256,256]{1,0:T(8,128)(2,1)S(1)}, u32[]{:S(2)}, u32[]{:S(2)}) collective-permute-start(bf16[256,256]{1,0:T(8,128)(2,1)S(1)} %get-tuple-element.334), channel_id=1, source_target_pairs={{0,3},{1,0},{2,1},{3,2},{4,7},{5,4},{6,5},{7,6},{8,11},{9,8},{10,9... | collective-permute-start | bytes 393224 | tf_op jit(solution)/shard_map/ppermute | solution.py:26
  97.0 1.9 %collective-permute-done.2 = bf16[256,256]{1,0:T(8,128)(2,1)S(1)} collective-permute-done((bf16[256,256]{1,0:T(8,128)(2,1)S(1)}, bf16[256,256]{1,0:T(8,128)(2,1)S(1)}, u32[]{:S(2)}, u32[]{:S(2)}) %collective-permute-start.2) | collective-permute-done | bytes 131104 | tf_op jit(solution)/shard_map/ppermute | solution.py:26
  99.1 9.5 %all-gather.3 = bf16[4,1,256]{2,1,0:T(2,128)(2,1)S(1)} all-gather(bf16[1,1,256]{2,1,0:T(2,128)(2,1)S(1)} %reshape.325), channel_id=1, replica_groups=mesh['slides'=2,'tiles'=4,'heads'=4] {'heads'}, dimensions={0}, use_global_device_ids=true | all-gather | bytes 2560 | tf_op jit(solution)/shard_map/all_gather | solution.py:183
  112.2 1.9 %constant_dynamic-slice_fusion.3 = bf16[1024,256]{1,0:T(8,128)(2,1)} fusion(bf16[2048,256]{1,0:T(8,128)(2,1)} %constant_dynamic-update-slice_fusion, s32[]{:T(128)S(6)} %select_n.37), kind=kLoop, calls=%fused_computation.92 | loop fusion | bytes 1048580 | tf_op jit(solution)/shard_map/jit(_roll_dynamic)/dynamic_slice | solution.py:28
  114.1 9.0 %while.35 = (s32[]{:T(128)}, f32[512,2]{0,1:T(2,128)S(1)}, f32[512,2]{0,1:T(2,128)S(1)}, f32[512,128]{0,1:T(8,128)S(1)}, bf16[4,256]{1,0:T(4,128)(2,1)S(1)}, /*i...) while((s32[]{:T(128)}, f32[512,2]{0,1:T(2,128)S(1)}, ...), condition=%wide.region_5.6_spmd.clone, body=%wide.region_2.5_spmd.clone.sunk | while | flops 103357440 | bytes 5174392 | solution.py:193
  123.8 13.4 %all-gather = f32[2048,2]{0,1:T(2,128)S(1)} all-gather(f32[512,2]{0,1:T(2,128)S(1)} %get-tuple-element.226), channel_id=2, replica_groups=mesh['slides'=2,'tiles'=4,'heads'=4] {'tiles'}, dimensions={0}, use_global_device_ids=true | all-gather | bytes 20480 | tf_op jit(solution)/shard_map/all_gather | solution.py:38
  137.2 13.2 %all-gather.1 = f32[2048,2]{0,1:T(2,128)S(1)} all-gather(f32[512,2]{0,1:T(2,128)S(1)} %get-tuple-element.227), channel_id=3, replica_groups=mesh['slides'=2,'tiles'=4,'heads'=4] {'tiles'}, dimensions={0}, use_global_device_ids=true | all-gather | bytes 20480 | tf_op jit(solution)/shard_map/all_gather | solution.py:38
  151.6 2.0 %reshape.318 = f32[4,512,128]{1,0,2:T(4,128)S(1)} reshape(f32[2048,128]{0,1:T(8,128)} %all-gather.6.cloned.1.call-done) | data formatting | bytes 2097152 | tf_op jit(solution)/shard_map/all_gather | solution.py:38
  153.6 1.2 while.34
  (134 shorter events, 25.1 us)
Async XLA Ops:
  6.5 1.4 copy-start
  6.5 145.0 %all-gather.6.cloned.1.call-start = ((), (), s32[]{:S(2)}) async-start(), calls=%async_computation | async-start | bytes 1310720 | tf_op jit(solution)/shard_map/all_gather | solution.py:38
  9.1 7.7 %copy-start.7 = (s32[1,3]{1,0:T(1,128)S(1)}, s32[1,3]{1,0:T(1,128)}, u32[]{:S(2)}) copy-start(s32[1,3]{1,0:T(1,128)} %param.23) | copy-start | bytes 40
  14.4 5.2 %collective-permute-start = (bf16[1,2,4096]{2,1,0:T(2,128)(2,1)S(1)}, bf16[1,2,4096]{2,1,0:T(2,128)(2,1)S(1)}, u32[]{:S(2)}, u32[]{:S(2)}) collective-permute-start(bf16[1,2,4096]{2,1,0:T(2,128)(2,1)S(1)} %pad_maximum_fusion.3), channel_id=1, source_target_pairs={{0,1},{1,2},{2,3},{3,4},{4,5},{5,6},{6,7},{7,8},{8,9},{9,10},{10,1... | collective-permute-start | bytes 49160 | tf_op jit(solution)/shard_map/ppermute | solution.py:34
  26.0 13.1 %copy-start.6 = (bf16[4,9,16,32]{3,2,1,0:T(8,128)(2,1)S(1)}, bf16[4,9,16,32]{3,2,1,0:T(8,128)(2,1)}, u32[]{:S(2)}) copy-start(bf16[4,9,16,32]{3,2,1,0:T(8,128)(2,1)} %param.16) | copy-start | bytes 110596
  62.2 10.1 %collective-permute-start.1 = (bf16[1,2,4096]{2,0,1:T(2,128)(2,1)S(1)}, bf16[1,2,4096]{2,0,1:T(2,128)(2,1)S(1)}, u32[]{:S(2)}, u32[]{:S(2)}) collective-permute-start(bf16[1,2,4096]{2,0,1:T(2,128)(2,1)S(1)} %pad_maximum_fusion.2), channel_id=1, source_target_pairs={{0,1},{1,2},{2,3},{3,4},{4,5},{5,6},{6,7},{7,8},{8,9},{9,10},{10,1... | collective-permute-start | bytes 49160 | tf_op jit(solution)/shard_map/ppermute | solution.py:34
  78.5 4.8 %copy-start.5 = (bf16[4,9,32,64]{3,2,1,0:T(8,128)(2,1)S(1)}, bf16[4,9,32,64]{3,2,1,0:T(8,128)(2,1)}, u32[]{:S(2)}) copy-start(bf16[4,9,32,64]{3,2,1,0:T(8,128)(2,1)} %param.17) | copy-start | bytes 442372
  88.7 19.9 %copy-start.2 = (bf16[512,128]{1,0:T(8,128)(2,1)S(1)}, bf16[512,128]{1,0:T(8,128)(2,1)}, u32[]{:S(2)}) copy-start(bf16[512,128]{1,0:T(8,128)(2,1)} %param.20) | copy-start | bytes 393220
  88.8 20.0 %copy-start.3 = (bf16[256,128]{1,0:T(8,128)(2,1)S(1)}, bf16[256,128]{1,0:T(8,128)(2,1)}, u32[]{:S(2)}) copy-start(bf16[256,128]{1,0:T(8,128)(2,1)} %param.19) | copy-start | bytes 196612
  88.8 20.0 %copy-start.4 = (bf16[256,128]{1,0:T(8,128)(2,1)S(1)}, bf16[256,128]{1,0:T(8,128)(2,1)}, u32[]{:S(2)}) copy-start(bf16[256,128]{1,0:T(8,128)(2,1)} %param.18) | copy-start | bytes 196612
  94.0 4.9 %collective-permute-start.2 = (bf16[256,256]{1,0:T(8,128)(2,1)S(1)}, bf16[256,256]{1,0:T(8,128)(2,1)S(1)}, u32[]{:S(2)}, u32[]{:S(2)}) collective-permute-start(bf16[256,256]{1,0:T(8,128)(2,1)S(1)} %get-tuple-element.334), channel_id=1, source_target_pairs={{0,3},{1,0},{2,1},{3,2},{4,7},{5,4},{6,5},{7,6},{8,11},{9,8},{10,9... | collective-permute-start | bytes 393224 | tf_op jit(solution)/shard_map/ppermute | solution.py:26
  98.9 10.5 %collective-permute-start.3 = (bf16[512,256]{1,0:T(8,128)(2,1)S(1)}, bf16[512,256]{1,0:T(8,128)(2,1)S(1)}, u32[]{:S(2)}, u32[]{:S(2)}) collective-permute-start(bf16[512,256]{1,0:T(8,128)(2,1)S(1)} %pad_maximum_fusion), channel_id=1, source_target_pairs={{0,2},{1,3},{2,0},{3,1},{4,6},{5,7},{6,4},{7,5},{8,10},{9,11},{10,... | collective-permute-start | bytes 786440 | tf_op jit(solution)/shard_map/ppermute | solution.py:26
  123.1 0.7 copy-start.1
  151.6 2.0 %slice-start = ((f32[2048,128]{0,1:T(8,128)}), f32[512,128]{0,1:T(8,128)S(1)}, s32[]{:S(2)}) async-start(f32[2048,128]{0,1:T(8,128)} %all-gather.6.cloned.1.call-done), calls=%async_computation.1 | async-start | bytes 524288 | tf_op jit(solution)/shard_map/slice | solution.py:39
Sparse Core Ops, SparseCore 0:
  123.9 27.6 all-gather.5
